TPU v7x, 256 devices: a whole 4x4x8 slice. The times are simulated.
256 devices in a mesh: seq: 32 (over x, z), head: 8 (over y, core).
Axes of the slice: x: 4, y: 4, z: 8, core: 2. Of those that a mesh axis runs over, the one named last changes fastest.
Arguments:
- queries: bfloat16 [4096, 8192], P('seq', 'head'), may hold values from -250 to 250
- key_vectors: bfloat16 [4096, 1024], P('seq', 'head'), may hold values from -250 to 250
- value_vectors: bfloat16 [4096, 1024], P('seq', 'head'), may hold values from -20 to 20
- positions: int32 [4096], P('seq'), may hold values from 0 to 2047, as said below
- query_map: float32 [64, 128, 128], P('head'), may hold values from -0.5 to 0.5
- key_map: float32 [8, 128, 128], P('head'), may hold values from -0.5 to 0.5
Outputs:
- grad_queries: float32 [4096, 8192], P('seq', 'head')
- grad_keys: float32 [4096, 1024], P('seq', 'head')
- grad_values: float32 [4096, 1024], P('seq', 'head')
- query_map_grad: float32 [64, 128, 128], P('head')
- key_map_grad: float32 [8, 128, 128], P('head')
Inputs may be any that keep to these rules, and one draw needn't show every extreme that they name: positions[0] is 0, and each later position is either 0 (a document begins) or one more than the position before it; the slab holds at most 4 documents, and one of them is exactly 2048 tokens long.
All inputs are finite; a program needn't handle non-finite values.
Results may differ from a plain program's by a relative error of at most 0.0025.
Values may be sent and summed in bfloat16 or wider, within the bound.
No kernel may reach another device: no remote copies, remote signals or barrier semaphores. Data moves between devices by JAX's collectives and lax.ppermute only.
A program may use at most 64 MiB of HBM per device.

v0:
```python
import math
import jax
import jax.numpy as jnp
from jax import lax
from jax.sharding import PartitionSpec as P

HIGHEST = lax.Precision.HIGHEST
NEGATIVE = -1e30
epsilon = 1e-06


def entering(value, axis, join, neutral, backward):
    count, mine = (lax.axis_size(axis), lax.axis_index(axis))
    pieces = jax.tree.map(lambda part: lax.all_gather(part, axis), value)
    if backward:
        pieces = jax.tree.map(lambda part: part[::-1], pieces)
        mine = count - 1 - mine
    running = jax.tree.map(
        lambda part, zero: jnp.full_like(part, 0) + jnp.asarray(zero, part.dtype), value, neutral
    )

    def lap(position, running):
        longer = join(running, jax.tree.map(lambda part: part[position], pieces))
        return jax.tree.map(lambda new, old: jnp.where(position < mine, new, old), longer, running)

    return lax.fori_loop(0, count - 1, lap, running)


def feature_map(logits):
    return jnp.concatenate(
        [jax.nn.softmax(logits, axis=-1), jax.nn.softmax(-logits, axis=-1)], axis=-1
    )


def feature_back(phi, grad_phi, half_width):
    upper = phi[..., :half_width]
    lower = phi[..., half_width:]
    grad_up = grad_phi[..., :half_width]
    grad_low = grad_phi[..., half_width:]
    upper_part = upper * (grad_up - jnp.sum(upper * grad_up, axis=-1, keepdims=True))
    lower_part = lower * (grad_low - jnp.sum(lower * grad_low, axis=-1, keepdims=True))
    return upper_part - lower_part


def chain_states(earlier, later):
    carried = 1.0 - later[2]
    return (
        later[0] + carried * earlier[0],
        later[1] + carried * earlier[1],
        jnp.maximum(earlier[2], later[2]),
    )


def on_device(queries, key_vectors, value_vectors, positions, query_map, key_map):
    tok_rows = queries.shape[0]
    n_group = query_map.shape[0]
    head_dim = key_vectors.shape[1]
    half_width = query_map.shape[2]
    feat_width = 2 * half_width
    my_index = lax.axis_index("seq")
    row_base = my_index * tok_rows
    row_index = row_base + jnp.arange(tok_rows, dtype=jnp.int32)
    starts = row_index - positions
    last_start = starts[-1]
    q_heads = queries.reshape(tok_rows, n_group, head_dim)
    scaling = 1.0 / math.sqrt(head_dim)
    key_float = key_vectors.astype(jnp.float32)
    value_float = value_vectors.astype(jnp.float32)
    key_logits = jnp.dot(key_float, key_map[0], precision=HIGHEST)
    key_phi = feature_map(key_logits)
    initial = (
        jnp.full((n_group, tok_rows), NEGATIVE, jnp.float32),
        jnp.zeros((n_group, tok_rows), jnp.float32),
        jnp.zeros((n_group, tok_rows, head_dim), jnp.float32),
        jnp.zeros((feat_width, head_dim), jnp.float32),
        jnp.zeros((feat_width,), jnp.float32),
    )
    key_block = lax.all_gather(key_vectors, "seq", axis=0, tiled=True)
    value_block = lax.all_gather(value_vectors, "seq", axis=0, tiled=True)
    block_len = key_block.shape[0]
    key_index = jnp.arange(block_len, dtype=jnp.int32)
    visible = (key_index[None, :] <= row_index[:, None]) & (key_index[None, :] >= starts[:, None])

    def update(current):
        run_max, row_sum, summed, state_sum, norm_sums = current
        scores = (
            jnp.einsum("tgd,nd->gtn", q_heads, key_block, preferred_element_type=jnp.float32)
            * scaling
        )
        scores = jnp.where(visible[None], scores, NEGATIVE)
        new_max = jnp.maximum(run_max, jnp.max(scores, axis=-1))
        weights = jnp.where(visible[None], jnp.exp(scores - new_max[..., None]), 0.0)
        row_sum = jnp.sum(weights, axis=-1)
        summed = jnp.einsum(
            "gtn,nd->gtd",
            weights.astype(jnp.bfloat16),
            value_block,
            preferred_element_type=jnp.float32,
        )
        return (new_max, row_sum, summed, state_sum, norm_sums)

    run_max, row_sum, summed, state_sum, norm_sums = lax.cond(
        jnp.any(visible), update, lambda current: current, initial
    )
    held_teacher = jnp.transpose(summed / row_sum[..., None], (1, 0, 2))
    query_float = q_heads.astype(jnp.float32)
    query_logits = jnp.einsum("tgd,gdf->tgf", query_float, query_map, precision=HIGHEST)
    query_phi = feature_map(query_logits)
    visible_rows = (
        (row_index[None, :] <= row_index[:, None]) & (row_index[None, :] >= starts[:, None])
    ).astype(jnp.float32)
    crossing = (starts < row_base).astype(jnp.float32)
    keeping = (starts == last_start).astype(jnp.float32)
    fresh_doc = (last_start >= row_base).astype(jnp.float32).reshape(1)
    kept_phi = key_phi * keeping[:, None]
    state_local = jnp.dot(kept_phi.T, value_float, precision=HIGHEST)
    norms_local = jnp.sum(kept_phi, axis=0)
    state_in, norms_in, unused = entering(
        (state_local, norms_local, fresh_doc),
        "seq",
        chain_states,
        (jnp.zeros_like(state_local), jnp.zeros_like(norms_local), jnp.zeros((1,), jnp.float32)),
        False,
    )
    inner = jnp.einsum("tgf,jf->gtj", query_phi, key_phi, precision=HIGHEST) * visible_rows[None]
    numer = jnp.einsum("gtj,jd->tgd", inner, value_float, precision=HIGHEST)
    numer = numer + crossing[:, None, None] * jnp.einsum(
        "tgf,fd->tgd", query_phi, state_in, precision=HIGHEST
    )
    denom = jnp.sum(inner, axis=-1).T + crossing[:, None] * jnp.einsum(
        "tgf,f->tg", query_phi, norms_in, precision=HIGHEST
    )
    outputs = numer / denom[..., None]
    error = outputs - held_teacher
    grad_numer = error / denom[..., None]
    grad_denom = -jnp.sum(error * outputs, axis=-1) / denom
    mixing = (
        jnp.einsum("tgd,jd->gtj", grad_numer, value_float, precision=HIGHEST)
        + grad_denom.T[:, :, None]
    ) * visible_rows[None]
    grad_qphi = jnp.einsum("gtj,jf->tgf", mixing, key_phi, precision=HIGHEST)
    grad_qphi = grad_qphi + crossing[:, None, None] * (
        jnp.einsum("tgd,fd->tgf", grad_numer, state_in, precision=HIGHEST)
        + grad_denom[..., None] * norms_in
    )
    crossing_phi = query_phi * crossing[:, None, None]
    back_local = jnp.einsum("tgf,tgd->fd", crossing_phi, grad_numer, precision=HIGHEST)
    back_norms = jnp.einsum("tgf,tg->f", crossing_phi, grad_denom, precision=HIGHEST)
    back_in, back_norms_in, unused_flag = entering(
        (back_local, back_norms, fresh_doc),
        "seq",
        chain_states,
        (jnp.zeros_like(back_local), jnp.zeros_like(back_norms), jnp.zeros((1,), jnp.float32)),
        True,
    )
    grad_kphi = jnp.einsum("gtj,tgf->jf", mixing, query_phi, precision=HIGHEST)
    grad_kphi = grad_kphi + keeping[:, None] * (
        jnp.dot(value_float, back_in.T, precision=HIGHEST) + back_norms_in[None, :]
    )
    grad_values = jnp.einsum("gtj,tgd->jd", inner, grad_numer, precision=HIGHEST)
    grad_values = grad_values + keeping[:, None] * jnp.dot(key_phi, back_in, precision=HIGHEST)
    query_dlogit = feature_back(query_phi, grad_qphi, half_width)
    key_dlogit = feature_back(key_phi, grad_kphi, half_width)
    grad_queries = jnp.einsum("tgf,gdf->tgd", query_dlogit, query_map, precision=HIGHEST).reshape(
        tok_rows, n_group * head_dim
    )
    grad_keys = jnp.dot(key_dlogit, key_map[0].T, precision=HIGHEST)
    local_qmap = jnp.einsum("tgd,tgf->gdf", query_float, query_dlogit, precision=HIGHEST)
    local_kmap = jnp.dot(key_float.T, key_dlogit, precision=HIGHEST)[None]
    clip_limit = 0.25 * math.sqrt((n_group + 1) * lax.axis_size("head") * head_dim * half_width)
    summed_qmap, summed_kmap = lax.psum((local_qmap, local_kmap), "seq")
    squared = lax.psum(
        jnp.sum(summed_qmap * summed_qmap) + jnp.sum(summed_kmap * summed_kmap), "head"
    )
    factor = jnp.minimum(1.0, clip_limit / (jnp.sqrt(squared) + epsilon))
    query_map_grad = factor * summed_qmap
    key_map_grad = factor * summed_kmap
    return (grad_queries, grad_keys, grad_values, query_map_grad, key_map_grad)


def solution(mesh):
    placed = (
        P("seq", "head"),
        P("seq", "head"),
        P("seq", "head"),
        P("seq"),
        P("head", None, None),
        P("head", None, None),
    )
    return jax.shard_map(
        on_device,
        mesh=mesh,
        in_specs=placed,
        out_specs=(
            P("seq", "head"),
            P("seq", "head"),
            P("seq", "head"),
            P("head", None, None),
            P("head", None, None),
        ),
        check_vma=False,
    )
```

profile of v0, /device:TPU:1, one launch (start us, length us, event | category | flops | bytes accessed | tf_op | source)
XLA Modules:
  0.0 715.1 jit_solution(13117342215060472636)
XLA Ops:
  14.3 39.5 %all-gather.4 = f32[32,1,256]{2,1,0:T(1,128)S(1)} all-gather(f32[1,1,256]{2,1,0:T(1,128)S(1)} %bitcast.184), channel_id=3, replica_groups=mesh['seq'=32,'head'=8] {'seq'}, dimensions={0}, use_global_device_ids=true | all-gather | bytes 33792 | tf_op jit(solution)/shard_map/all_gather | solution.py:14
  53.8 1.8 copy.60
  59.4 57.9 %all-reduce = f32[32]{0:T(128)S(1)} all-reduce(f32[32]{0:T(128)S(1)} %dynamic-update-slice), channel_id=1, replica_groups=mesh['seq'=32,'head'=8] {'seq'}, use_global_device_ids=true, to_apply=%add | all-reduce | flops 32 | bytes 256
  120.7 2.0 convolution_bitcast_fusion.3
  122.7 39.8 %all-gather.13.cloned.1.call-done = bf16[4096,128]{1,0:T(8,128)(2,1)} async-done(((bf16[128,128]{1,0:T(8,128)(2,1)}), bf16[4096,128]{1,0:T(8,128)(2,1)}) %all-gather.13.cloned.1.call-update) | async-done | bytes 1048592 | tf_op jit(solution)/shard_map/all_gather | solution.py:79
  162.5 12.8 %conditional.1 = (f32[8,128]{1,0:T(8,128)S(1)}, f32[8,128,128]{1,2,0:T(8,128)}) conditional(s32[]{:T(128)} %convert_element_type.26, () %tuple.45, (pred[128,4096]{0,1:T(8,128)(4,1)S(1)}, bf16[4096,128]{1,0:T(8,128)(2,1)}, bf16[128,8,128]{0,2,1:T(8,128)(2,1)}, bf16[4096,128]{1,0:T(8,128)(2,1)}) %tuple.46), branch_computations={%region_13.14_spmd, %region_14.17_spmd} | conditional | flops 2202008576 | bytes 59007020 | solution.py:102
  162.5 3.8 fusion
  166.4 4.8 fusion.3
  171.2 4.0 fusion.2
  175.4 70.9 %all-gather.15.cloned.1.call-done = f32[8192,128]{1,0:T(8,128)} async-done(((f32[256,128]{1,0:T(8,128)}), f32[8192,128]{1,0:T(8,128)}) %all-gather.15.cloned.1.call-update) | async-done | bytes 4194320 | tf_op jit(solution)/shard_map/all_gather | solution.py:14
  246.3 90.0 %while.32 = (s32[]{:T(128)}, f32[256,128]{1,0:T(8,128)S(1)}, f32[256]{0:T(256)S(1)}, s32[]{:T(128)}, f32[32,256,128]{2,1,0:T(8,128)}, /*index=5*/f32[32,1]{0,1:T...) while((s32[]{:T(128)}, f32[256,128]{1,0:T(8,128)S(1)}, f32[256]{0:T(256)S(1)}, s32[]{:T(128)}, ...), condition=%wide.region_10.11_spmd.clone, body=%wide.region_9.10_spmd.clone.sunk | while | flops 132101 | bytes 398487 | solution.py:26
  262.1 1.6 fusion.106
  337.0 2.1 multiply_reduce_fusion.3
  339.0 1.7 convolution_bitcast_fusion.6
  341.8 32.8 %all-gather.5 = f32[32,1,256]{2,1,0:T(1,128)S(1)} all-gather(f32[1,1,256]{2,1,0:T(1,128)S(1)} %convolution_bitcast_fusion.10), channel_id=5, replica_groups=mesh['seq'=32,'head'=8] {'seq'}, dimensions={0}, use_global_device_ids=true | all-gather | bytes 33792 | tf_op jit(solution)/shard_map/all_gather | solution.py:14
  375.7 1.6 convolution_bitcast_fusion.7
  379.7 2.4 convolution_bitcast_fusion.1
  382.1 37.8 %all-gather.17.cloned.1.call-done = f32[8192,128]{1,0:T(8,128)} async-done(((f32[256,128]{1,0:T(8,128)}), f32[8192,128]{1,0:T(8,128)}) %all-gather.17.cloned.1.call-update) | async-done | bytes 4194320 | tf_op jit(solution)/shard_map/all_gather | solution.py:14
  419.9 4.6 rev.9
  424.5 109.9 %while.33 = (s32[]{:T(128)}, f32[256,128]{1,0:T(8,128)S(1)}, f32[256]{0:T(256)S(1)}, s32[]{:T(128)}, f32[32,256,128]{2,1,0:T(8,128)}, /*index=5*/f32[32,1]{0,1:T(1,128)S(1)}, f32[32,256]{1,0:T(8,128)}, s32[]{:T(128)}, s32[]{:T(128)}) while((s32[]{:T(128)}, f32[256,128]{1,0:T(8,128)S(1)}, f32[256]{0:T(256)S(1)}, s32[]{:T(128)}, ...), condition=%wide.region_21.22_spmd.clone, body=%wide.region_20.21_spmd.clone.sunk | while | flops 132101 | bytes 398487 | solution.py:26
  540.4 139.9 %all-reduce.4.cloned.1.call-done = (f32[8,128,128]{1,2,0:T(8,128)}, f32[1,128,128]{1,2,0:T(8,128)}) async-done(((f32[8,128,128]{1,2,0:T(8,128)}, f32[1,128,128]{1,2,0:T(8,128)}), (f32[8,128,128]{1,2,0:T(8,128)}, f32[1,128,128]{1,2,0:T(8,128)})) %all-reduce.4.cloned.1.call-update) | async-done | bytes 589840 | tf_op jit(solution)/shard_map/psum | solution.py:171
  681.7 1.8 multiply_reduce_fusion
  684.8 1.8 fusion.44
  686.6 17.6 %psum.23 = f32[]{:T(128)} all-reduce(f32[]{:T(128)S(6)} %add.151), channel_id=1, replica_groups=mesh['seq'=32,'head'=8] {'head'}, use_global_device_ids=true, to_apply=%region_28.29 | all-reduce | flops 1 | bytes 8 | tf_op jit(solution)/shard_map/psum | solution.py:172
  (315 shorter events, 225.9 us)
Async XLA Ops:
  7.2 110.2 %copy-start = (f32[8,128,128]{2,1,0:T(8,128)S(1)}, f32[8,128,128]{2,1,0:T(8,128)}, u32[]{:S(2)}) copy-start(f32[8,128,128]{2,1,0:T(8,128)} %param.16) | copy-start | bytes 1572868
  7.2 115.5 %all-gather.11.cloned.1.call-start = ((), (), s32[]{:S(2)}) async-start(), calls=%async_computation | async-start | bytes 1081344 | tf_op jit(solution)/shard_map/all_gather | solution.py:78
  7.9 154.6 %all-gather.13.cloned.1.call-start = ((), (), s32[]{:S(2)}) async-start(), calls=%async_computation.1 | async-start | bytes 1081344 | tf_op jit(solution)/shard_map/all_gather | solution.py:79
  8.7 237.7 %all-gather.15.cloned.1.call-start = ((), (), s32[]{:S(2)}) async-start(), calls=%async_computation.2 | async-start | bytes 4325376 | tf_op jit(solution)/shard_map/all_gather | solution.py:14
  13.5 406.4 %all-gather.17.cloned.1.call-start = ((), (), s32[]{:S(2)}) async-start(), calls=%async_computation.3 | async-start | bytes 4325376 | tf_op jit(solution)/shard_map/all_gather | solution.py:14
  162.5 212.7 %copy-start.1 = (bf16[128,128]{1,0:T(8,128)(2,1)S(1)}, bf16[128,128]{1,0:T(8,128)(2,1)}, u32[]{:S(2)}) copy-start(bf16[128,128]{1,0:T(8,128)(2,1)} %param.14) | copy-start | bytes 98308
  162.5 3.8 copy-start.2
  340.7 339.6 %all-reduce.4.cloned.1.call-start = ((), (), s32[]{:S(2)}) async-start(), calls=%async_computation.4 | async-start | bytes 1179648 | tf_op jit(solution)/shard_map/psum | solution.py:171
Sparse Core Ops, SparseCore 0:
  10.6 75.4 all-gather.10
  88.7 73.7 all-gather.12
  165.1 81.1 all-gather.14
  340.8 79.0 all-gather.16
  537.3 142.9 all-reduce.3
where the time goes:
time: 720 us; the launch traced here: 715 us
  waiting for transfers between devices  290 us (40%)
  other arithmetic  190 us (26%)
  blocking collectives  148 us (21%)
  local copies, waits for them, and re-layouts  34.3 us (5%)
  matrix products  34.1 us (5%)
  between operations  17.4 us (2%)
    psum x1, waiting for transfers between devices, on_device(): summed_qmap, summed_kmap = lax.psum((local_qmap, local_kmap), 'seq')  140 us
    select_n x124, other arithmetic, lap(): jnp.where(position < mine, new, old)  140 us
    all_gather x2, waiting for transfers between devices, entering(): pieces = jax.tree.map(lambda part: lax.all_gather(part, axis), value)  109 us
    all_gather x2, blocking collectives, entering(): pieces = jax.tree.map(lambda part: lax.all_gather(part, axis), value)  72.3 us
    unnamed x1, blocking collectives  57.9 us
    all_gather x1, waiting for transfers between devices, on_device(): value_block = lax.all_gather(value_vectors, 'seq', axis=0, tiled=True)  39.8 us
    sub x62, other arithmetic, chain_states(): carried = 1.0 - later[2]  36.6 us
    dynamic_slice x62, local copies, waits for them, and re-layouts, lap(): longer = join(running, jax.tree.map(lambda part: part[position], pieces))  21.9 us
  transfers between devices with their start and end apart: 5, of which 4 were waited for; matrix products, arithmetic and copies ran while one was open for 6% of the time, Pallas kernels for 0%

commit v1 on v0

--- a/solution.py
+++ b/solution.py
@@ -76,7 +76,11 @@
         jnp.zeros((feat_width,), jnp.float32),
     )
     key_block = lax.all_gather(key_vectors, "seq", axis=0, tiled=True)
-    value_block = lax.all_gather(value_vectors, "seq", axis=0, tiled=True)
+    many = lax.axis_size("seq")
+    entries = [many if c == 0 else 1 for c in range(value_vectors.ndim)]
+    value_block = lax.all_to_all(
+        jnp.tile(value_vectors, entries), "seq", split_axis=0, concat_axis=0, tiled=True
+    )
     block_len = key_block.shape[0]
     key_index = jnp.arange(block_len, dtype=jnp.int32)
     visible = (key_index[None, :] <= row_index[:, None]) & (key_index[None, :] >= starts[:, None])

time: 720 us -> 649 us (0.901)
  waiting for transfers between devices: 290 us -> 195 us
  starting transfers between devices: 0.2 us -> 12.2 us
  blocking collectives: 148 us -> 156 us
    all_gather x2, waiting for transfers between devices: 109 us -> 55 us  [entering(): pieces = jax.tree.map(lambda part: lax.all_gather(part, axis), value)]
    all_gather x1 -> x0, waiting for transfers between devices: 39.8 us -> none  [on_device(): value_block = lax.all_gather(value_vectors, 'seq', axis=0, tiled=True)]
    all_to_all x0 -> x1, starting transfers between devices: none -> 12 us  [on_device(): lax.all_to_all(jnp.tile(value_vectors, entries), 'seq', split_axis=0, con...]
    all_gather x2, blocking collectives: 72.3 us -> 80.3 us  [entering(): pieces = jax.tree.map(lambda part: lax.all_gather(part, axis), value)]
  transfers between devices with their start and end apart: 5 -> 5, of which waited for: 4 -> 3; matrix products, arithmetic and copies ran while one was open for 6% -> 7% of each run, Pallas kernels for 0% -> 0%
where the time goes in v1:
time: 649 us; the launch traced here: 644 us
  waiting for transfers between devices  195 us (30%)
  other arithmetic  190 us (29%)
  blocking collectives  156 us (24%)
  local copies, waits for them, and re-layouts  36.8 us (6%)
  matrix products  35.2 us (5%)
  between operations  17.4 us (3%)
  starting transfers between devices  12.2 us (2%)
    select_n x124, other arithmetic, lap(): jnp.where(position < mine, new, old)  140 us
    psum x1, waiting for transfers between devices, on_device(): summed_qmap, summed_kmap = lax.psum((local_qmap, local_kmap), 'seq')  140 us
    all_gather x2, blocking collectives, entering(): pieces = jax.tree.map(lambda part: lax.all_gather(part, axis), value)  80.3 us
    unnamed x1, blocking collectives  58.5 us
    all_gather x2, waiting for transfers between devices, entering(): pieces = jax.tree.map(lambda part: lax.all_gather(part, axis), value)  55 us
    sub x62, other arithmetic, chain_states(): carried = 1.0 - later[2]  36.6 us
    dynamic_slice x62, local copies, waits for them, and re-layouts, lap(): longer = join(running, jax.tree.map(lambda part: part[position], pieces))  22.3 us
    psum x1, blocking collectives, on_device(): lax.psum(jnp.sum(summed_qmap * summed_qmap) + jnp.sum(summed_kmap * summe...  17.6 us
  transfers between devices with their start and end apart: 5, of which 3 were waited for; matrix products, arithmetic and copies ran while one was open for 7% of the time, Pallas kernels for 0%

profile of v1, /device:TPU:1, one launch (start us, length us, event | category | flops | bytes accessed | tf_op | source)
XLA Modules:
  0.0 644.3 jit_solution(7642527102291334190)
XLA Ops:
  12.7 2.0 tile.2
  14.7 12.0 %all-to-all-start = ((bf16[32,128,128]{2,1,0:T(8,128)(2,1)}), bf16[32,128,128]{2,1,0:T(8,128)(2,1)}, u32[]{:S(2)}, u32[]{:S(2)}) async-start(bf16[32,128,128]{2,1,0:T(8,128)(2,1)} %tile.2), calls=%async_computation | async-start | bytes 2097152 | tf_op jit(solution)/shard_map/all_to_all | solution.py:81
  27.4 1.8 copy.60
  31.2 48.5 %all-gather.4 = f32[32,1,256]{2,1,0:T(1,128)S(1)} all-gather(f32[1,1,256]{2,1,0:T(1,128)S(1)} %bitcast.185), channel_id=3, replica_groups=mesh['seq'=32,'head'=8] {'seq'}, dimensions={0}, use_global_device_ids=true | all-gather | bytes 33792 | tf_op jit(solution)/shard_map/all_gather | solution.py:14
  81.7 58.5 %all-reduce = f32[32]{0:T(128)S(1)} all-reduce(f32[32]{0:T(128)S(1)} %dynamic-update-slice), channel_id=1, replica_groups=mesh['seq'=32,'head'=8] {'seq'}, use_global_device_ids=true, to_apply=%add | all-reduce | flops 32 | bytes 256
  143.6 2.0 convolution_bitcast_fusion.3
  145.6 13.8 %conditional.1 = (f32[8,128]{1,0:T(8,128)S(1)}, f32[8,128,128]{1,2,0:T(8,128)}) conditional(s32[]{:T(128)} %convert_element_type.26, () %tuple.45, (pred[128,4096]{0,1:T(8,128)(4,1)S(1)}, bf16[4096,128]{1,0:T(8,128)(2,1)}, bf16[128,8,128]{0,2,1:T(8,128)(2,1)}, bf16[32,128,128]{2,1,0:T(8,128)(2,1)}) %tuple.46), branch_computations={%region_13.14_spmd, %region_14.17_spmd} | conditional | flops 2202008576 | bytes 54812688 | solution.py:106
  145.6 3.8 fusion
  149.4 4.0 fusion.2
  153.4 6.0 fusion.3
  159.4 13.3 %all-gather.12.cloned.1.call-done = f32[8192,128]{1,0:T(8,128)} async-done(((f32[256,128]{1,0:T(8,128)}), f32[8192,128]{1,0:T(8,128)}) %all-gather.12.cloned.1.call-update) | async-done | bytes 4194320 | tf_op jit(solution)/shard_map/all_gather | solution.py:14
  172.7 90.2 %while.32 = (s32[]{:T(128)}, f32[256,128]{1,0:T(8,128)S(1)}, f32[256]{0:T(256)S(1)}, s32[]{:T(128)}, f32[32,256,128]{2,1,0:T(8,128)}, /*index=5*/f32[32,1]{0,1:T...) while((s32[]{:T(128)}, f32[256,128]{1,0:T(8,128)S(1)}, f32[256]{0:T(256)S(1)}, s32[]{:T(128)}, ...), condition=%wide.region_10.11_spmd.clone, body=%wide.region_9.10_spmd.clone.sunk | while | flops 132101 | bytes 398487 | solution.py:26
  263.5 2.1 multiply_reduce_fusion.3
  265.6 1.6 convolution_bitcast_fusion.6
  268.4 31.8 %all-gather.5 = f32[32,1,256]{2,1,0:T(1,128)S(1)} all-gather(f32[1,1,256]{2,1,0:T(1,128)S(1)} %convolution_bitcast_fusion.10), channel_id=5, replica_groups=mesh['seq'=32,'head'=8] {'seq'}, dimensions={0}, use_global_device_ids=true | all-gather | bytes 33792 | tf_op jit(solution)/shard_map/all_gather | solution.py:14
  301.2 1.6 convolution_bitcast_fusion.7
  305.2 2.4 convolution_bitcast_fusion.1
  307.6 41.7 %all-gather.14.cloned.1.call-done = f32[8192,128]{1,0:T(8,128)} async-done(((f32[256,128]{1,0:T(8,128)}), f32[8192,128]{1,0:T(8,128)}) %all-gather.14.cloned.1.call-update) | async-done | bytes 4194320 | tf_op jit(solution)/shard_map/all_gather | solution.py:14
  349.3 4.6 rev.9
  353.9 109.8 %while.33 = (s32[]{:T(128)}, f32[256,128]{1,0:T(8,128)S(1)}, f32[256]{0:T(256)S(1)}, s32[]{:T(128)}, f32[32,256,128]{2,1,0:T(8,128)}, /*index=5*/f32[32,1]{0,1:T(1,128)S(1)}, f32[32,256]{1,0:T(8,128)}, s32[]{:T(128)}, s32[]{:T(128)}) while((s32[]{:T(128)}, f32[256,128]{1,0:T(8,128)S(1)}, f32[256]{0:T(256)S(1)}, s32[]{:T(128)}, ...), condition=%wide.region_21.22_spmd.clone, body=%wide.region_20.21_spmd.clone.sunk | while | flops 132101 | bytes 398487 | solution.py:26
  469.7 139.8 %all-reduce.4.cloned.1.call-done = (f32[8,128,128]{1,2,0:T(8,128)}, f32[1,128,128]{1,2,0:T(8,128)}) async-done(((f32[8,128,128]{1,2,0:T(8,128)}, f32[1,128,128]{1,2,0:T(8,128)}), (f32[8,128,128]{1,2,0:T(8,128)}, f32[1,128,128]{1,2,0:T(8,128)})) %all-reduce.4.cloned.1.call-update) | async-done | bytes 589840 | tf_op jit(solution)/shard_map/psum | solution.py:175
  609.5 1.8 multiply_reduce_fusion
  614.0 1.8 fusion.43
  615.8 17.6 %psum.23 = f32[]{:T(128)} all-reduce(f32[]{:T(128)S(6)} %add.151), channel_id=1, replica_groups=mesh['seq'=32,'head'=8] {'head'}, use_global_device_ids=true, to_apply=%region_28.29 | all-reduce | flops 1 | bytes 8 | tf_op jit(solution)/shard_map/psum | solution.py:176
  (313 shorter events, 227.1 us)
Async XLA Ops:
  7.2 133.1 %copy-start = (f32[8,128,128]{2,1,0:T(8,128)S(1)}, f32[8,128,128]{2,1,0:T(8,128)}, u32[]{:S(2)}) copy-start(f32[8,128,128]{2,1,0:T(8,128)} %param.16) | copy-start | bytes 1572868
  7.2 138.4 %all-gather.10.cloned.1.call-start = ((), (), s32[]{:S(2)}) async-start(), calls=%async_computation.1 | async-start | bytes 1081344 | tf_op jit(solution)/shard_map/all_gather | solution.py:78
  7.9 164.8 %all-gather.12.cloned.1.call-start = ((), (), s32[]{:S(2)}) async-start(), calls=%async_computation.2 | async-start | bytes 4325376 | tf_op jit(solution)/shard_map/all_gather | solution.py:14
  14.7 130.9 %all-to-all-start = ((bf16[32,128,128]{2,1,0:T(8,128)(2,1)}), bf16[32,128,128]{2,1,0:T(8,128)(2,1)}, u32[]{:S(2)}, u32[]{:S(2)}) async-start(bf16[32,128,128]{2,1,0:T(8,128)(2,1)} %tile.2), calls=%async_computation | async-start | bytes 2097152 | tf_op jit(solution)/shard_map/all_to_all | solution.py:81
  26.7 322.6 %all-gather.14.cloned.1.call-start = ((), (), s32[]{:S(2)}) async-start(), calls=%async_computation.3 | async-start | bytes 4325376 | tf_op jit(solution)/shard_map/all_gather | solution.py:14
  145.6 155.2 %copy-start.1 = (bf16[128,128]{1,0:T(8,128)(2,1)S(1)}, bf16[128,128]{1,0:T(8,128)(2,1)}, u32[]{:S(2)}) copy-start(bf16[128,128]{1,0:T(8,128)(2,1)} %param.14) | copy-start | bytes 98308
  267.3 342.2 %all-reduce.4.cloned.1.call-start = ((), (), s32[]{:S(2)}) async-start(), calls=%async_computation.4 | async-start | bytes 1179648 | tf_op jit(solution)/shard_map/psum | solution.py:175
Sparse Core Ops, SparseCore 0:
  10.6 78.2 all-gather.9
  91.5 81.1 all-gather.11
  267.4 81.8 all-gather.13
  466.6 142.8 all-reduce.3
